TPU v7x, 512 devices: a whole 4x4x16 slice. The times are simulated.
512 devices in a mesh: section: 32 (over z, core), seq: 16 (over x, y).
Axes of the slice: x: 4, y: 4, z: 16, core: 2. Of those that a mesh axis runs over, the one named last changes fastest.
Arguments:
- layer_input: bfloat16 [32, 3, 4096, 768], P('section', None, 'seq'), may hold values from -6 to 6
- grad_out: bfloat16 [32, 3, 4096, 768], P('section', None, 'seq'), may hold values from -6 to 6
- gate_weight: bfloat16 [768, 768], P('seq'), may hold values from -0.21875 to 0.21875
- mix_in_right: bfloat16 [64, 64, 64], P('seq'), may hold values from -0.75 to 0.75
- mix_in_left: bfloat16 [64, 64, 64], P('seq'), may hold values from -0.75 to 0.75
- mix_out_left: bfloat16 [64, 64, 64], P('seq'), may hold values from -0.75 to 0.75
- mix_out_right: bfloat16 [64, 64, 64], P('seq'), may hold values from -0.75 to 0.75
- kernel: bfloat16 [4096, 768], P('seq'), may hold values from -5 to 5
Outputs:
- input_grad: bfloat16 [32, 3, 4096, 768], P('section', None, 'seq')
- weight_grad: float32 [768, 768], P('seq')
- kernel_grad: bfloat16 [4096, 768], P('seq')
All inputs are finite; a program needn't handle non-finite values.
Results may differ from a plain program's by a relative error of at most 0.007.
Values may be sent and summed in bfloat16 or wider, within the bound.
A program may use at most 64 MiB of HBM per device.

v0:
```python
import math

import jax
import jax.numpy as jnp
from jax import lax
from jax.sharding import PartitionSpec as P

BATCH = 3
SEQ = 4096


def contract(form, left, right):
    return jnp.einsum(form, left, right, preferred_element_type=jnp.float32)


def forward_middle(spread, left_in, left_out, kern):
    second_mixed = contract("ija,baid->bijd", left_in, spread)
    weighted = (second_mixed * kern).astype(jnp.bfloat16)
    third_mixed = contract("ikj,bijd->bikd", left_out, weighted).astype(jnp.bfloat16)
    return (second_mixed, third_mixed)


def backward_middle(back_spread, second_mixed, left_in, left_out, kern):
    back_second = contract("ikj,bkid->bijd", left_out, back_spread)
    kernel_sum = jnp.sum(second_mixed * back_second, axis=0)
    back_weighted = (back_second * kern).astype(jnp.bfloat16)
    back_first = contract("ija,bijd->biad", left_in, back_weighted).astype(jnp.bfloat16)
    return (kernel_sum, back_first)


def local(
    layer_input,
    grad_out,
    gate_weight,
    mix_in_right,
    mix_in_left,
    mix_out_left,
    mix_out_right,
    kernel,
):
    count_batch = layer_input.shape[1]
    token_rows = layer_input.shape[2]
    width = layer_input.shape[3]
    groups = mix_in_right.shape[0]
    block_size = mix_in_right.shape[1]
    replicas = lax.axis_size("section")
    kern = kernel.reshape(groups, block_size, width).astype(jnp.float32)
    acts = layer_input[0].reshape(count_batch, groups, block_size, width)
    flat_input = layer_input[0].reshape(count_batch * token_rows, width)
    upstream = grad_out[0].reshape(count_batch * token_rows, width).astype(jnp.float32)
    weights = lax.all_gather(gate_weight, "seq", axis=0, tiled=True)
    preact = jnp.dot(flat_input, weights, preferred_element_type=jnp.float32)
    sigma = jax.nn.sigmoid(preact)
    swish = preact * sigma
    slope = sigma * (1.0 + preact * (1.0 - sigma))
    mix_grad = (
        (upstream * swish).astype(jnp.bfloat16).reshape(count_batch, groups, block_size, width)
    )
    first_mixed = contract("aic,bacd->baid", mix_in_right, acts).astype(jnp.bfloat16)
    back_third = contract("kmi,bkmd->bkid", mix_out_right, mix_grad).astype(jnp.bfloat16)
    spread = lax.all_to_all(first_mixed, "seq", split_axis=2, concat_axis=1, tiled=True)
    second_mixed, third_mixed = forward_middle(spread, mix_in_left, mix_out_left, kern)
    returned = lax.all_to_all(third_mixed, "seq", split_axis=2, concat_axis=1, tiled=True)
    back_spread = lax.all_to_all(back_third, "seq", split_axis=2, concat_axis=1, tiled=True)
    kernel_sum, back_first = backward_middle(
        back_spread, second_mixed, mix_in_left, mix_out_left, kern
    )
    back_return = lax.all_to_all(back_first, "seq", split_axis=2, concat_axis=1, tiled=True)
    mixed = contract("kmi,bikd->bkmd", mix_out_right, returned).reshape(
        count_batch * token_rows, width
    )
    gate_grad = (upstream * mixed * slope).astype(jnp.bfloat16)
    gate_part = lax.dot_general(
        gate_grad, weights, (((1,), (1,)), ((), ())), preferred_element_type=jnp.float32
    )
    weight_scale = 1.0 / math.sqrt(replicas * BATCH * SEQ)
    kernel_scale = 1.0 / math.sqrt(replicas * BATCH)
    term = lax.dot_general(
        flat_input, gate_grad, (((0,), (0,)), ((), ())), preferred_element_type=jnp.float32
    )
    weight_local = lax.psum_scatter(term * weight_scale, "seq", scatter_dimension=0, tiled=True)
    weight_grad, kernel_total = lax.psum((weight_local, kernel_sum * kernel_scale), "section")
    mix_part = contract("aic,biad->bacd", mix_in_right, back_return).reshape(
        count_batch * token_rows, width
    )
    input_grad = (
        (gate_part + mix_part).astype(jnp.bfloat16).reshape(1, count_batch, token_rows, width)
    )
    kernel_grad = kernel_total.astype(jnp.bfloat16).reshape(groups * block_size, width)
    return (input_grad, weight_grad, kernel_grad)


def solution(mesh):
    placed = (
        P("section", None, "seq", None),
        P("section", None, "seq", None),
        P("seq", None),
        P("seq", None, None),
        P("seq", None, None),
        P("seq", None, None),
        P("seq", None, None),
        P("seq", None),
    )
    return jax.shard_map(
        local,
        mesh=mesh,
        in_specs=placed,
        out_specs=(P("section", None, "seq", None), P("seq", None), P("seq", None)),
        check_vma=False,
    )
```

profile of v0, /device:TPU:1, one launch (start us, length us, event | category | flops | bytes accessed | tf_op | source)
XLA Modules:
  0.0 457.5 jit_solution(12352171297710613128)
XLA Ops:
  7.2 1.3 copy-done
  8.4 1.3 fusion.9
  9.7 1.9 copy.54
  11.7 7.7 %all-to-all-start = ((bf16[3,4,64,768]{3,1,0,2:T(4,128)(2,1)}), bf16[3,4,64,768]{3,1,0,2:T(4,128)(2,1)S(1)}, u32[]{:S(2)}, u32[]{:S(2)}) async-start(bf16[3,4,64,768]{3,1,0,2:T(4,128)(2,1)} %copy.54), calls=%async_computation | async-start | bytes 2359296 | tf_op jit(solution)/shard_map/all_to_all | solution.py:61
  20.2 0.9 convert.3
  21.1 14.0 %all-to-all-done = bf16[3,4,64,768]{3,1,0,2:T(4,128)(2,1)S(1)} async-done(((bf16[3,4,64,768]{3,1,0,2:T(4,128)(2,1)}), bf16[3,4,64,768]{3,1,0,2:T(4,128)(2,1)S(1)}, u32[]{:S(2)}, u32[]{:S(2)}) %all-to-all-start) | async-done | bytes 1179680 | tf_op jit(solution)/shard_map/all_to_all | solution.py:61
  35.6 1.2 all_to_all.55
  36.8 1.8 fusion.23
  40.1 22.7 %all_to_all.72 = bf16[3,4,64,768]{3,1,0,2:T(4,128)(2,1)S(1)} all-to-all(bf16[3,4,64,768]{3,1,0,2:T(4,128)(2,1)S(1)} %copy.56), channel_id=1, replica_groups=mesh['section'=32,'seq'=16] {'seq'}, dimensions={2} | all-to-all | bytes 2359296 | tf_op jit(solution)/shard_map/all_to_all | solution.py:63
  62.8 1.5 copy.98
  64.3 3.1 all_to_all.59
  67.5 1.7 convolution_bitcast_fusion
  69.2 1.6 copy.58
  70.8 19.2 %all-gather.2.cloned.1.call-done = bf16[768,768]{1,0:T(8,128)(2,1)} async-done(((bf16[48,768]{1,0:T(8,128)(2,1)}), bf16[768,768]{1,0:T(8,128)(2,1)}) %all-gather.2.cloned.1.call-update) | async-done | bytes 1179664 | tf_op jit(solution)/shard_map/all_gather | solution.py:51
  90.0 5.1 %fusion.1 = (bf16[768,768]{1,0:T(8,128)(2,1)S(1)}, bf16[768,768]{1,0:T(8,128)(2,1)}) fusion(f32[3,4,64,768]{3,2,1,0:T(8,128)} %copy.58, bf16[1,3,256,768]{3,2,1,0:T(8,128)(2,1)} %param.9, bf16[768,768]{1,0:T(8,128)(2,1)S(1)} %bitcast.123, bf16[768,768]{1,0:T(8,128)(2,1)} %all-gather.2.cloned.1.call-done), kind=kOutput, calls=%fused_computation.3 | convolution fusion | flops 914227200 | bytes 8257536 | tf_op jit(solution)/shard_map/dot_general | solution.py:52
  95.1 1.1 copy-done.7
  96.2 2.5 multiply_bitcast_fusion
  98.7 3.1 copy.86
  101.8 1.8 fusion.7
  104.5 20.8 %all_to_all.73 = bf16[3,4,64,768]{3,1,0,2:T(4,128)(2,1)S(1)} all-to-all(bf16[3,4,64,768]{3,1,0,2:T(4,128)(2,1)S(1)} %copy.61), channel_id=1, replica_groups=mesh['section'=32,'seq'=16] {'seq'}, dimensions={2} | all-to-all | bytes 2359296 | tf_op jit(solution)/shard_map/all_to_all | solution.py:64
  125.3 1.5 copy.97
  126.9 3.2 all_to_all.63
  130.0 2.8 fusion.5
  133.4 1.9 copy.65
  135.3 4.3 all-to-all-start.3
  139.6 1.0 broadcast_multiply_fusion
  140.6 101.4 %all-reduce.4 = bf16[4,64,768]{2,1,0:T(8,128)(2,1)} all-reduce(f32[4,64,768]{2,1,0:T(8,128)} %broadcast_multiply_fusion), channel_id=1, replica_groups=mesh['section'=32,'seq'=16] {'section'}, use_global_device_ids=true, to_apply=%region_3.0 | all-reduce | flops 196608 | bytes 1179648 | tf_op jit(solution)/shard_map/psum | solution.py:82
  242.8 1.4 convolution_bitcast_fusion.1
  244.4 1.8 copy.87
  246.2 3.8 fusion.3
  250.0 199.2 %all-reduce.3.cloned.1.call-done = f32[48,768]{0,1:T(8,128)} async-done(((f32[48,768]{0,1:T(8,128)}), f32[48,768]{0,1:T(8,128)}) %all-reduce.3.cloned.1.call-update) | async-done | bytes 147472 | tf_op jit(solution)/shard_map/psum | solution.py:82
  449.2 1.8 copy.69
  (30 shorter events, 5.2 us)
Async XLA Ops:
  7.2 1.3 copy-start
  11.7 8.5 %copy-start.4 = (bf16[256,768]{1,0:T(8,128)(2,1)S(1)}, bf16[256,768]{1,0:T(8,128)(2,1)}, u32[]{:S(2)}) copy-start(bf16[256,768]{1,0:T(8,128)(2,1)} %param.15) | copy-start | bytes 1179652
  11.7 23.5 %all-to-all-start = ((bf16[3,4,64,768]{3,1,0,2:T(4,128)(2,1)}), bf16[3,4,64,768]{3,1,0,2:T(4,128)(2,1)S(1)}, u32[]{:S(2)}, u32[]{:S(2)}) async-start(bf16[3,4,64,768]{3,1,0,2:T(4,128)(2,1)} %copy.54), calls=%async_computation | async-start | bytes 2359296 | tf_op jit(solution)/shard_map/all_to_all | solution.py:61
  19.4 70.6 %all-gather.2.cloned.1.call-start = ((), (), s32[]{:S(2)}) async-start(), calls=%async_computation.5 | async-start | bytes 1253376 | tf_op jit(solution)/shard_map/all_gather | solution.py:51
  20.1 224.2 %reduce-scatter.4.cloned.1.call-start = ((), (), s32[]{:S(2)}) async-start(), calls=%async_computation.7 | async-start | bytes 2506752
  36.8 1.8 copy-start.1
  36.8 1.8 copy-start.5
  95.1 1.1 copy-start.7
  130.0 2.8 copy-start.2
  130.0 2.8 copy-start.6
  135.3 4.3 copy-start.3
  135.3 106.7 %all-to-all-start.3 = ((bf16[3,4,64,768]{3,1,0,2:T(4,128)(2,1)}), bf16[3,4,64,768]{3,1,0,2:T(4,128)(2,1)S(1)}, u32[]{:S(2)}, u32[]{:S(2)}) async-start(bf16[3,4,64,768]{3,1,0,2:T(4,128)(2,1)} %copy.65), calls=%async_computation.3 | async-start | bytes 2359296 | tf_op jit(solution)/shard_map/all_to_all | solution.py:68
  139.6 309.6 %all-reduce.3.cloned.1.call-start = ((), (), s32[]{:S(2)}) async-start(), calls=%async_computation.6 | async-start | bytes 786432 | tf_op jit(solution)/shard_map/psum | solution.py:82
Sparse Core Ops, SparseCore 0:
  23.3 66.6 all-gather.1
  101.9 97.3 reduce-scatter.3
  246.3 202.7 all-reduce.2
where the time goes:
time: 459 us; the launch traced here: 457 us
  waiting for transfers between devices  233 us (51%)
  blocking collectives  145 us (32%)
  local copies, waits for them, and re-layouts  28.3 us (6%)
  matrix products  23.3 us (5%)
  between operations  13.9 us (3%)
  starting transfers between devices  12.1 us (3%)
    psum x1, waiting for transfers between devices, local(): lax.psum((weight_local, kernel_sum * kernel_scale), 'section')  199 us
    psum x1, blocking collectives, local(): lax.psum((weight_local, kernel_sum * kernel_scale), 'section')  101 us
    all_to_all x1, blocking collectives, local(): lax.all_to_all(third_mixed, 'seq', split_axis=2, concat_axis=1, tiled=True)  22.7 us
    all_to_all x1, blocking collectives, local(): lax.all_to_all(back_third, 'seq', split_axis=2, concat_axis=1, tiled=True)  20.8 us
    all_gather x1, waiting for transfers between devices, local(): weights = lax.all_gather(gate_weight, 'seq', axis=0, tiled=True)  19.2 us
    all_to_all x1, waiting for transfers between devices, local(): lax.all_to_all(first_mixed, 'seq', split_axis=2, concat_axis=1, tiled=True)  14 us
    dot_general x8, matrix products, contract(): return jnp.einsum(form, left, right, preferred_element_type=jnp.float32)  11.8 us
  transfers between devices with their start and end apart: 5, of which 3 were waited for; matrix products, arithmetic and copies ran while one was open for 6% of the time, Pallas kernels for 0%

commit v1 on v0

v1 whole, which is shorter than its diff:
```python
import math

import jax
import jax.numpy as jnp
from jax import lax
from jax.experimental import pallas as pl
from jax.experimental.pallas import tpu as pltpu
from jax.sharding import PartitionSpec as P

MESH = pl.DeviceIdType.MESH
BF16 = jnp.bfloat16
F32 = jnp.float32

PEERS = 16
BATCH = 3
ROWS = 256
WIDTH = 768
HALF = WIDTH // 2
TILE = 256
SHARD = WIDTH // PEERS
CHUNK = 512

FIRST, THIRD, BACK_THIRD, BACK_FIRST = 0, 1, 2, 3
IN_RIGHT, IN_LEFT, OUT_LEFT, OUT_RIGHT = 0, 1, 2, 3


def product(left, right, contract=((1,), (0,))):
    return lax.dot_general(left, right, (contract, ((), ())), preferred_element_type=F32)


def rows_of(index, size):
    return pl.ds(pl.multiple_of(index * size, size), size)


def mixer(
    x_any,
    g_any,
    w_any,
    in_right,
    in_left,
    out_left,
    out_right,
    kern_any,
    grad_any,
    weight_out,
    kernel_out,
    x,
    g,
    w,
    kern,
    mats,
    sent,
    got,
    second,
    slope,
    gate,
    grad,
    ksum,
    term,
    term_out,
    term_in,
    term_sent,
    term_got,
    kern_out,
    kern_in,
    z_sent,
    z_got,
    z_all,
    local_sem,
    send_sem,
    recv_sem,
    one_send,
    one_recv,
):
    section = lax.axis_index("section")
    me = lax.axis_index("seq")
    core = lax.rem(section, 2)
    level = lax.div(section, 2)
    other = 1 - core
    sibling = (2 * level + other, me)

    def seq_peer(step):
        return lax.rem(me + step, PEERS)

    def z_peer(step):
        return lax.rem(level + step, PEERS)

    my_half = pl.ds(pl.multiple_of(core * HALF, HALF), HALF)
    other_half = pl.ds(pl.multiple_of(other * HALF, HALF), HALF)
    loads = [
        pltpu.make_async_copy(x_any, x, local_sem.at[0]),
        pltpu.make_async_copy(
            w_any.at[:, my_half], w.at[rows_of(me, SHARD), my_half], local_sem.at[1]
        ),
        pltpu.make_async_copy(g_any, g, local_sem.at[2]),
        pltpu.make_async_copy(kern_any, kern, local_sem.at[3]),
    ]
    for load in loads:
        load.start()

    barrier = pltpu.get_barrier_semaphore()

    @pl.loop(1, PEERS)
    def _(step):
        pl.semaphore_signal(barrier, inc=1, device_id=(section, seq_peer(step)), device_id_type=MESH)
        pl.semaphore_signal(
            barrier, inc=1, device_id=(2 * z_peer(step) + core, me), device_id_type=MESH
        )

    pl.semaphore_signal(barrier, inc=1, device_id=sibling, device_id_type=MESH)

    row = lax.broadcasted_iota(jnp.int32, (ROWS, ROWS), 0)
    col = lax.broadcasted_iota(jnp.int32, (ROWS, ROWS), 1)
    small_row = lax.broadcasted_iota(jnp.int32, (64, ROWS), 0)
    small_col = lax.broadcasted_iota(jnp.int32, (64, ROWS), 1)
    order = jnp.where(col == (row & 3) * 64 + (row >> 2), 1.0, 0.0).astype(BF16)
    repeat = jnp.where(small_row == (small_col & 63), 1.0, 0.0).astype(BF16)
    spread = jnp.where(small_row == (small_col >> 4) * 4 + (small_col & 3), 1.0, 0.0).astype(BF16)
    on_block = (row >> 6) == (col >> 6)
    on_spread = (row >> 6) == ((col >> 2) & 3)
    for slot, factor in ((IN_RIGHT, in_right), (OUT_LEFT, out_left)):
        blocks = jnp.where(on_block, product(factor[...], repeat), 0.0).astype(BF16)
        matrix = product(order, blocks)
        mats[slot] = matrix.astype(BF16)
        mats[slot + 4] = matrix.T.astype(BF16)
    for slot, factor in ((IN_LEFT, in_left), (OUT_RIGHT, out_right)):
        matrix = jnp.where(on_spread, product(factor[...], spread), 0.0)
        mats[slot] = matrix.astype(BF16)
        mats[slot + 4] = matrix.T.astype(BF16)

    pl.semaphore_wait(barrier, 2 * (PEERS - 1) + 1)

    def exchange(which, b):
        @pl.loop(1, PEERS)
        def _(step):
            to = seq_peer(step)
            pltpu.make_async_remote_copy(
                sent.at[which, pl.ds(pl.multiple_of(b * ROWS + to * 16, 16), 16)],
                got.at[which, pl.ds(pl.multiple_of(b * ROWS + me * 16, 16), 16)],
                send_sem.at[which, b],
                recv_sem.at[which, b],
                device_id=(section, to),
                device_id_type=MESH,
            ).start()

        mine = pl.ds(pl.multiple_of(b * ROWS + me * 16, 16), 16)
        got[which, mine] = sent[which, mine]

    def exchanged(which, b):
        span = pl.ds(pl.multiple_of(b * ROWS, ROWS), ROWS - 16)
        return pltpu.make_async_remote_copy(
            sent.at[which, span],
            got.at[which, span],
            send_sem.at[which, b],
            recv_sem.at[which, b],
            device_id=(section, seq_peer(1)),
            device_id_type=MESH,
        )

    def single(source, target, slot, to):
        return pltpu.make_async_remote_copy(
            source, target, one_send.at[slot], one_recv.at[slot], device_id=to, device_id_type=MESH
        )

    tiles = [slice(at, at + TILE) for at in range(0, WIDTH, TILE)]

    loads[1].wait()

    @pl.loop(1, PEERS)
    def _(step):
        piece = w.at[rows_of(me, SHARD), my_half]
        single(piece, piece, 0, (section, seq_peer(step))).start()

    loads[0].wait()

    @pl.loop(0, BATCH)
    def _(b):
        here = rows_of(b, ROWS)
        for tile in tiles:
            sent[FIRST, here, tile] = product(mats[IN_RIGHT], x[here, tile]).astype(BF16)
        exchange(FIRST, b)

    most = w.at[pl.ds(0, WIDTH - SHARD), my_half]
    gathered = single(most, most, 0, (section, seq_peer(1)))
    gathered.wait_recv()
    half = w.at[:, my_half]
    paired = single(half, half, 1, sibling)
    paired.start()
    paired.wait_recv()
    loads[2].wait()
    loads[3].wait()

    @pl.loop(0, BATCH)
    def _(b):
        here = rows_of(b, ROWS)
        for tile in tiles:
            preact = product(x[here, :], w[:, tile])
            sigma = jax.nn.sigmoid(preact)
            upstream = g[here, tile].astype(F32)
            slope[here, tile] = upstream * (sigma * (1.0 + preact * (1.0 - sigma)))
            mix_grad = (upstream * (preact * sigma)).astype(BF16)
            sent[BACK_THIRD, here, tile] = product(mats[OUT_RIGHT + 4], mix_grad).astype(BF16)

    @pl.loop(0, BATCH)
    def _(b):
        here = rows_of(b, ROWS)
        exchanged(FIRST, b).wait_recv()
        for tile in tiles:
            mixed_in = product(mats[IN_LEFT], got[FIRST, here, tile])
            second[here, tile] = mixed_in
            weighted = (mixed_in * kern[:, tile].astype(F32)).astype(BF16)
            sent[THIRD, here, tile] = product(mats[OUT_LEFT], weighted).astype(BF16)
        exchange(THIRD, b)

    @pl.loop(0, BATCH)
    def _(b):
        exchange(BACK_THIRD, b)

    @pl.loop(0, BATCH)
    def _(b):
        here = rows_of(b, ROWS)
        exchanged(THIRD, b).wait_recv()
        for tile in tiles:
            mixed = product(mats[OUT_RIGHT], got[THIRD, here, tile])
            gate[here, tile] = (mixed * slope[here, tile]).astype(BF16)
        for tile in tiles:
            slope[here, tile] = product(gate[here, :], w[tile, :], ((1,), (1,)))

    for tile in tiles:
        term_out[tile, :] = product(x[:, tile], gate[:, other_half], ((0,), (0,))).astype(BF16)
    swapped = single(term_out, term_in, 2, sibling)
    swapped.start()
    for tile in tiles:
        term[tile, :] = product(x[:, tile], gate[:, my_half], ((0,), (0,)))
    swapped.wait_recv()
    term_sent[...] = (term[...] + term_in[...].astype(F32)).astype(BF16)

    @pl.loop(1, PEERS)
    def _(step):
        to = seq_peer(step)
        single(
            term_sent.at[rows_of(to, SHARD)], term_got.at[rows_of(me, SHARD)], 3, (section, to)
        ).start()

    term_got[rows_of(me, SHARD)] = term_sent[rows_of(me, SHARD)]

    ksum[...] = jnp.zeros_like(ksum)

    @pl.loop(0, BATCH)
    def _(b):
        here = rows_of(b, ROWS)
        exchanged(BACK_THIRD, b).wait_recv()
        for tile in tiles:
            back_second = product(mats[OUT_LEFT + 4], got[BACK_THIRD, here, tile])
            ksum[:, tile] += second[here, tile] * back_second
            back_weighted = (back_second * kern[:, tile].astype(F32)).astype(BF16)
            sent[BACK_FIRST, here, tile] = product(mats[IN_LEFT + 4], back_weighted).astype(BF16)
        exchange(BACK_FIRST, b)

    kern_out[...] = ksum[rows_of(other, ROWS // 2)].astype(BF16)
    kern_swap = single(kern_out, kern_in, 4, sibling)
    kern_swap.start()

    spans = pl.ds(0, WIDTH - SHARD)
    scattered = single(term_sent.at[spans], term_got.at[spans], 3, (section, seq_peer(1)))
    scattered.wait_recv()
    rows = term_got[0:SHARD].astype(F32)
    for source in range(1, PEERS):
        rows += term_got[source * SHARD : (source + 1) * SHARD].astype(F32)
    z_sent[:, :, HALF:] = jnp.zeros((PEERS, 16, CHUNK - HALF), BF16)
    for part in range(9):
        down, across = (part // 3) * 16, (part % 3) * 128
        z_sent[part, :, HALF:] = rows[down : down + 16, across : across + 128].astype(BF16)

    kern_swap.wait_recv()
    half_sum = ksum[rows_of(core, ROWS // 2)] + kern_in[...].astype(F32)
    for part in range(PEERS):
        down, across = (part // 2) * 16, (part % 2) * HALF
        z_sent[part, :, :HALF] = half_sum[down : down + 16, across : across + HALF].astype(BF16)

    @pl.loop(1, PEERS)
    def _(step):
        to = z_peer(step)
        single(z_sent.at[to], z_got.at[level], 5, (2 * to + core, me)).start()

    z_got[level] = z_sent[level]
    z_span = pl.ds(0, PEERS - 1)
    next_level = (2 * z_peer(1) + core, me)
    reduced = single(z_sent.at[z_span], z_got.at[z_span], 5, next_level)
    reduced.wait_recv()
    chunk = z_got[0].astype(F32)
    for source in range(1, PEERS):
        chunk += z_got[source].astype(F32)
    replicas = 2 * PEERS
    z_all[core, level, :, :HALF] = (chunk[:, :HALF] * (1.0 / math.sqrt(replicas * BATCH))).astype(BF16)
    z_all[core, level, :, HALF:] = (
        chunk[:, HALF:] * (1.0 / math.sqrt(replicas * BATCH * PEERS * ROWS))
    ).astype(BF16)

    @pl.loop(1, PEERS)
    def _(step):
        piece = z_all.at[core, level]
        single(piece, piece, 6, (2 * z_peer(step) + core, me)).start()

    stores = []
    for b in range(BATCH):
        here = slice(b * ROWS, (b + 1) * ROWS)
        exchanged(BACK_FIRST, b).wait_recv()
        for tile in tiles:
            mix_part = product(mats[IN_RIGHT + 4], got[BACK_FIRST, here, tile])
            grad[here, tile] = (slope[here, tile] + mix_part).astype(BF16)
        store = pltpu.make_async_copy(grad.at[here], grad_any.at[here], local_sem.at[4 + b])
        store.start()
        stores.append(store)

    z_rest = z_all.at[core, z_span]
    collected = single(z_rest, z_rest, 6, next_level)
    collected.wait_recv()
    z_half = z_all.at[core]
    z_swap = single(z_half, z_half, 7, sibling)
    z_swap.start()
    z_swap.wait_recv()
    for side in range(2):
        for part in range(PEERS):
            down, across = side * (ROWS // 2) + (part // 2) * 16, (part % 2) * HALF
            kernel_out[down : down + 16, across : across + HALF] = z_all[side, part, :, :HALF]
        for part in range(9):
            down, across = (part // 3) * 16, side * HALF + (part % 3) * 128
            weight_out[down : down + 16, across : across + 128] = z_all[side, part, :, HALF:].astype(F32)

    for store in stores:
        store.wait()
    for done in (gathered, paired, swapped, scattered, kern_swap, reduced, collected, z_swap):
        done.wait_send()
    for which in range(4):

        @pl.loop(0, BATCH)
        def _(b):
            exchanged(which, b).wait_send()


def local(
    layer_input,
    grad_out,
    gate_weight,
    mix_in_right,
    mix_in_left,
    mix_out_left,
    mix_out_right,
    kernel,
):
    tokens = BATCH * ROWS
    anywhere = pl.BlockSpec(memory_space=pl.ANY)
    inside = pl.BlockSpec(memory_space=pltpu.VMEM)
    input_grad, weight_grad, kernel_grad = pl.pallas_call(
        mixer,
        out_shape=(
            jax.ShapeDtypeStruct((tokens, WIDTH), BF16),
            jax.ShapeDtypeStruct((SHARD, WIDTH), F32),
            jax.ShapeDtypeStruct((ROWS, WIDTH), BF16),
        ),
        in_specs=[anywhere] * 3 + [inside] * 4 + [anywhere],
        out_specs=(anywhere, inside, inside),
        scratch_shapes=[
            pltpu.VMEM((tokens, WIDTH), BF16),
            pltpu.VMEM((tokens, WIDTH), BF16),
            pltpu.VMEM((WIDTH, WIDTH), BF16),
            pltpu.VMEM((ROWS, WIDTH), BF16),
            pltpu.VMEM((8, ROWS, ROWS), BF16),
            pltpu.VMEM((4, tokens, WIDTH), BF16),
            pltpu.VMEM((4, tokens, WIDTH), BF16),
            pltpu.VMEM((tokens, WIDTH), F32),
            pltpu.VMEM((tokens, WIDTH), F32),
            pltpu.VMEM((tokens, WIDTH), BF16),
            pltpu.VMEM((tokens, WIDTH), BF16),
            pltpu.VMEM((ROWS, WIDTH), F32),
            pltpu.VMEM((WIDTH, HALF), F32),
            pltpu.VMEM((WIDTH, HALF), BF16),
            pltpu.VMEM((WIDTH, HALF), BF16),
            pltpu.VMEM((WIDTH, HALF), BF16),
            pltpu.VMEM((WIDTH, HALF), BF16),
            pltpu.VMEM((ROWS // 2, WIDTH), BF16),
            pltpu.VMEM((ROWS // 2, WIDTH), BF16),
            pltpu.VMEM((PEERS, 16, CHUNK), BF16),
            pltpu.VMEM((PEERS, 16, CHUNK), BF16),
            pltpu.VMEM((2, PEERS, 16, CHUNK), BF16),
            pltpu.SemaphoreType.DMA((7,)),
            pltpu.SemaphoreType.DMA((4, BATCH)),
            pltpu.SemaphoreType.DMA((4, BATCH)),
            pltpu.SemaphoreType.DMA((8,)),
            pltpu.SemaphoreType.DMA((8,)),
        ],
        compiler_params=pltpu.CompilerParams(
            collective_id=0, has_side_effects=True, vmem_limit_bytes=52 << 20
        ),
    )(
        layer_input.reshape(tokens, WIDTH),
        grad_out.reshape(tokens, WIDTH),
        gate_weight,
        mix_in_right.reshape(ROWS, 64),
        mix_in_left.reshape(ROWS, 64),
        mix_out_left.reshape(ROWS, 64),
        mix_out_right.reshape(ROWS, 64),
        kernel,
    )
    return (input_grad.reshape(1, BATCH, ROWS, WIDTH), weight_grad, kernel_grad)


def solution(mesh):
    placed = (
        P("section", None, "seq", None),
        P("section", None, "seq", None),
        P("seq", None),
        P("seq", None, None),
        P("seq", None, None),
        P("seq", None, None),
        P("seq", None, None),
        P("seq", None),
    )
    return jax.shard_map(
        local,
        mesh=mesh,
        in_specs=placed,
        out_specs=(P("section", None, "seq", None), P("seq", None), P("seq", None)),
        check_vma=False,
    )
```

time: 459 us -> 116 us (0.25)
  waiting for transfers between devices: 233 us -> 0 us
  blocking collectives: 145 us -> 0 us
  Pallas kernels: 0 us -> 106 us
  matrix products: 23.3 us -> 0 us
  local copies, waits for them, and re-layouts: 28.3 us -> 8.99 us
  between operations: 13.9 us -> 0.66 us
  starting transfers between devices: 12.1 us -> 0 us
    psum x1 -> x0, waiting for transfers between devices: 199 us -> none  [local(): lax.psum((weight_local, kernel_sum * kernel_scale), 'section')]
    pallas_call x0 -> x1, Pallas kernels: none -> 106 us  [local(): pl.pallas_call(mixer, out_shape=(jax.ShapeDtypeStruct((tokens, WIDTH), BF...]
    psum x1 -> x0, blocking collectives: 101 us -> none  [local(): lax.psum((weight_local, kernel_sum * kernel_scale), 'section')]
    all_to_all x2 -> x0, blocking collectives: 43.5 us -> none  [the longest x1 22.7 us: local(): lax.all_to_all(third_mixed, 'seq', split_axis=2, concat_axis=1, tiled=True)]
    dot_general x11 -> x0, matrix products: 23.3 us -> none  [the longest x8 11.8 us: contract(): return jnp.einsum(form, left, right, preferred_element_type=jnp.float32)]
    all_gather x1 -> x0, waiting for transfers between devices: 19.2 us -> none  [local(): weights = lax.all_gather(gate_weight, 'seq', axis=0, tiled=True)]
    all_to_all x2 -> x0, waiting for transfers between devices: 14 us -> none  [the longest x1 14 us: local(): lax.all_to_all(first_mixed, 'seq', split_axis=2, concat_axis=1, tiled=True)]
    all_to_all x2 -> x0, starting transfers between devices: 12 us -> none  [the longest x1 7.71 us: local(): lax.all_to_all(first_mixed, 'seq', split_axis=2, concat_axis=1, tiled=True)]
  transfers between devices with their start and end apart: 5 -> 0, of which waited for: 3 -> 0; matrix products, arithmetic and copies ran while one was open for 6% -> 0% of each run, Pallas kernels for 0% -> 0%
where the time goes in v1:
time: 116 us; the launch traced here: 115 us
  Pallas kernels  106 us (91%)
  local copies, waits for them, and re-layouts  8.99 us (8%)
    pallas_call x1, Pallas kernels, local(): pl.pallas_call(mixer, out_shape=(jax.ShapeDtypeStruct((tokens, WIDTH), BF...  106 us
    unnamed x15, local copies, waits for them, and re-layouts  8.99 us

profile of v1, /device:TPU:1, one launch (start us, length us, event | category | flops | bytes accessed | tf_op | source)
XLA Modules:
  0.0 115.5 jit_solution(17382719329835787853)
XLA Ops:
  0.6 0.0 copy-start
  0.6 1.0 copy-done
  1.6 0.0 copy-start.1
  1.6 0.9 copy-done.1
  2.5 0.0 copy-start.2
  2.5 0.8 copy-done.2
  3.4 0.0 copy-start.3
  3.4 0.8 copy-done.3
  4.2 0.0 copy-start.4
  4.2 0.8 copy-done.4
  5.0 0.0 copy-start.5
  5.0 0.8 copy-done.5
  5.9 105.8 %shard_map.103 = (bf16[768,768]{1,0:T(8,128)(2,1)}, f32[48,768]{1,0:T(8,128)S(1)}, bf16[256,768]{1,0:T(8,128)(2,1)S(1)}) custom-call(bf16[768,768]{1,0:T(8,128)(2,1)} %bitcast.11, bf16[768,768]{1,0:T(8,128)(2,1)} %bitcast.12, bf16[48,768]{1,0:T(8,128)(2,1)S(1)} %copy-done.1, bf16[256,64]{1,0:T(8,128)(2,1)S(1)} %bitcast.7, bf16[256,64]{1,0:T(8,128)(2,1)S(1)} %bitcast.8, ...), custom_call_target="tpu_custom_call" | custom-call | tf_op jit(solution)/shard_map/pallas_call | solution.py:355
  111.7 2.4 %copy.14 = bf16[1,3,256,768]{3,2,1,0:T(8,128)(2,1)} copy(bf16[1,3,256,768]{3,2,1,0:T(8,128)(2,1)} %bitcast.13) | data formatting | bytes 2359296
  114.1 0.7 copy.15
  114.7 0.7 copy.16
Async XLA Ops:
  0.6 1.0 copy-start
  1.6 0.9 copy-start.1
  2.5 0.8 copy-start.2
  3.4 0.8 copy-start.3
  4.2 0.8 copy-start.4
  5.0 0.8 copy-start.5

commit v2 on v1

v2 whole, which is shorter than its diff:
```python
import math

import jax
import jax.numpy as jnp
from jax import lax
from jax.experimental import pallas as pl
from jax.experimental.pallas import tpu as pltpu
from jax.sharding import PartitionSpec as P

MESH = pl.DeviceIdType.MESH
BF16 = jnp.bfloat16
F32 = jnp.float32

PEERS = 16
BATCH = 3
ROWS = 256
WIDTH = 768
HALF = WIDTH // 2
TILE = 256
SHARD = WIDTH // PEERS

FIRST, THIRD, BACK_THIRD, BACK_FIRST = 0, 1, 2, 3
IN_RIGHT, IN_LEFT, OUT_LEFT, OUT_RIGHT = 0, 1, 2, 3


def product(left, right, contract=((1,), (0,))):
    return lax.dot_general(left, right, (contract, ((), ())), preferred_element_type=F32)


def rows_of(index, size):
    return pl.ds(pl.multiple_of(index * size, size), size)


def mixer(
    x_any,
    g_any,
    w_any,
    in_right_any,
    in_left_any,
    out_left_any,
    out_right_any,
    kern_any,
    grad,
    weight_out,
    kernel_out,
    x,
    g,
    w,
    kern,
    factors,
    mats,
    sent,
    got,
    second,
    slope,
    gate,
    ksum,
    term,
    term_out,
    term_in,
    term_sent,
    term_got,
    kern_out,
    kern_in,
    kern_sent,
    kern_got,
    kern_all,
    part_sent,
    part_got,
    part_all,
    local_sem,
    send_sem,
    recv_sem,
    one_send,
    one_recv,
):
    section = lax.axis_index("section")
    me = lax.axis_index("seq")
    core = lax.rem(section, 2)
    level = lax.div(section, 2)
    other = 1 - core
    sibling = (2 * level + other, me)

    def seq_peer(step):
        return lax.rem(me + step, PEERS)

    def z_peer(step):
        return lax.rem(level + step, PEERS)

    my_half = pl.ds(pl.multiple_of(core * HALF, HALF), HALF)
    other_half = pl.ds(pl.multiple_of(other * HALF, HALF), HALF)
    barrier = pltpu.get_barrier_semaphore()

    @pl.loop(1, PEERS)
    def _(step):
        pl.semaphore_signal(barrier, inc=1, device_id=(section, seq_peer(step)), device_id_type=MESH)
        pl.semaphore_signal(
            barrier, inc=1, device_id=(2 * z_peer(step) + core, me), device_id_type=MESH
        )

    pl.semaphore_signal(barrier, inc=1, device_id=sibling, device_id_type=MESH)

    loads = [
        pltpu.make_async_copy(source, target, local_sem.at[slot])
        for slot, (source, target) in enumerate(
            (
                (in_right_any, factors.at[IN_RIGHT]),
                (w_any.at[:, my_half], w.at[rows_of(me, SHARD), my_half]),
                (x_any, x),
                (in_left_any, factors.at[IN_LEFT]),
                (out_left_any, factors.at[OUT_LEFT]),
                (out_right_any, factors.at[OUT_RIGHT]),
                (g_any, g),
                (kern_any, kern),
            )
        )
    ]
    for load in loads:
        load.start()
    part_sent[...] = jnp.zeros_like(part_sent)
    row = lax.broadcasted_iota(jnp.int32, (ROWS, ROWS), 0)
    col = lax.broadcasted_iota(jnp.int32, (ROWS, ROWS), 1)
    small_row = lax.broadcasted_iota(jnp.int32, (64, ROWS), 0)
    small_col = lax.broadcasted_iota(jnp.int32, (64, ROWS), 1)
    order = jnp.where(col == (row & 3) * 64 + (row >> 2), 1.0, 0.0).astype(BF16)
    repeat = jnp.where(small_row == (small_col & 63), 1.0, 0.0).astype(BF16)
    spread = jnp.where(small_row == (small_col >> 4) * 4 + (small_col & 3), 1.0, 0.0).astype(BF16)
    on_block = (row >> 6) == (col >> 6)
    on_spread = (row >> 6) == ((col >> 2) & 3)

    def ordered(slot):
        blocks = jnp.where(on_block, product(factors[slot], repeat), 0.0).astype(BF16)
        matrix = product(order, blocks)
        mats[slot] = matrix.astype(BF16)
        mats[slot + 4] = matrix.T.astype(BF16)

    def spaced(slot):
        matrix = jnp.where(on_spread, product(factors[slot], spread), 0.0)
        mats[slot] = matrix.astype(BF16)
        mats[slot + 4] = matrix.T.astype(BF16)

    loads[0].wait()
    ordered(IN_RIGHT)
    loads[1].wait()
    loads[2].wait()
    pl.semaphore_wait(barrier, 2 * (PEERS - 1) + 1)

    def exchange(which, b):
        @pl.loop(1, PEERS)
        def _(step):
            to = seq_peer(step)
            pltpu.make_async_remote_copy(
                sent.at[which, pl.ds(pl.multiple_of(b * ROWS + to * 16, 16), 16)],
                got.at[which, pl.ds(pl.multiple_of(b * ROWS + me * 16, 16), 16)],
                send_sem.at[which, b],
                recv_sem.at[which, b],
                device_id=(section, to),
                device_id_type=MESH,
            ).start()

        mine = pl.ds(pl.multiple_of(b * ROWS + me * 16, 16), 16)
        got[which, mine] = sent[which, mine]

    def exchanged(which, b):
        span = pl.ds(pl.multiple_of(b * ROWS, ROWS), ROWS - 16)
        return pltpu.make_async_remote_copy(
            sent.at[which, span],
            got.at[which, span],
            send_sem.at[which, b],
            recv_sem.at[which, b],
            device_id=(section, seq_peer(1)),
            device_id_type=MESH,
        )

    def single(source, target, slot, to):
        return pltpu.make_async_remote_copy(
            source, target, one_send.at[slot], one_recv.at[slot], device_id=to, device_id_type=MESH
        )

    tiles = [slice(at, at + TILE) for at in range(0, WIDTH, TILE)]
    @pl.loop(1, PEERS)
    def _(step):
        piece = w.at[rows_of(me, SHARD), my_half]
        single(piece, piece, 0, (section, seq_peer(step))).start()
    @pl.loop(0, BATCH)
    def _(b):
        here = rows_of(b, ROWS)
        for tile in tiles:
            sent[FIRST, here, tile] = product(mats[IN_RIGHT], x[here, tile]).astype(BF16)
        exchange(FIRST, b)
    for load in loads[3:]:
        load.wait()
    spaced(IN_LEFT)
    ordered(OUT_LEFT)
    spaced(OUT_RIGHT)
    most = w.at[pl.ds(0, WIDTH - SHARD), my_half]
    gathered = single(most, most, 0, (section, seq_peer(1)))
    gathered.wait_recv()
    half = w.at[:, my_half]
    paired = single(half, half, 1, sibling)
    paired.start()
    paired.wait_recv()
    @pl.loop(0, BATCH)
    def _(b):
        here = rows_of(b, ROWS)
        for tile in tiles:
            preact = product(x[here, :], w[:, tile])
            sigma = jax.nn.sigmoid(preact)
            upstream = g[here, tile].astype(F32)
            slope[here, tile] = upstream * (sigma * (1.0 + preact * (1.0 - sigma)))
            mix_grad = (upstream * (preact * sigma)).astype(BF16)
            sent[BACK_THIRD, here, tile] = product(mats[OUT_RIGHT + 4], mix_grad).astype(BF16)
        exchange(BACK_THIRD, b)
    @pl.loop(0, BATCH)
    def _(b):
        here = rows_of(b, ROWS)
        exchanged(FIRST, b).wait_recv()
        for tile in tiles:
            mixed_in = product(mats[IN_LEFT], got[FIRST, here, tile])
            second[here, tile] = mixed_in
            weighted = (mixed_in * kern[:, tile].astype(F32)).astype(BF16)
            sent[THIRD, here, tile] = product(mats[OUT_LEFT], weighted).astype(BF16)
        exchange(THIRD, b)
    ksum[...] = jnp.zeros_like(ksum)

    def back(b):
        here = rows_of(b, ROWS)
        exchanged(BACK_THIRD, b).wait_recv()
        for tile in tiles:
            back_second = product(mats[OUT_LEFT + 4], got[BACK_THIRD, here, tile])
            ksum[:, tile] += second[here, tile] * back_second
            back_weighted = (back_second * kern[:, tile].astype(F32)).astype(BF16)
            sent[BACK_FIRST, here, tile] = product(mats[IN_LEFT + 4], back_weighted).astype(BF16)

    @pl.loop(0, BATCH - 1)
    def _(b):
        back(b)
        exchange(BACK_FIRST, b)

    back(BATCH - 1)
    kern_out[...] = ksum[rows_of(other, ROWS // 2)].astype(BF16)
    kern_swap = single(kern_out, kern_in, 4, sibling)
    kern_swap.start()
    kern_swap.wait_recv()
    half_sum = ksum[rows_of(core, ROWS // 2)] + kern_in[...].astype(F32)
    for part in range(PEERS):
        down, across = (part // 2) * 16, (part % 2) * HALF
        kern_sent[part] = half_sum[down : down + 16, across : across + HALF].astype(BF16)

    @pl.loop(1, PEERS)
    def _(step):
        to = z_peer(step)
        single(kern_sent.at[to], kern_got.at[level], 5, (2 * to + core, me)).start()

    kern_got[level] = kern_sent[level]
    @pl.loop(0, BATCH)
    def _(b):
        here = rows_of(b, ROWS)
        exchanged(THIRD, b).wait_recv()
        for tile in tiles:
            mixed = product(mats[OUT_RIGHT], got[THIRD, here, tile])
            gate[here, tile] = (mixed * slope[here, tile]).astype(BF16)
    for tile in tiles:
        term_out[tile, :] = product(x[:, tile], gate[:, other_half], ((0,), (0,))).astype(BF16)
    swapped = single(term_out, term_in, 2, sibling)
    swapped.start()
    for tile in tiles:
        term[tile, :] = product(x[:, tile], gate[:, my_half], ((0,), (0,)))
    swapped.wait_recv()
    term_sent[...] = (term[...] + term_in[...].astype(F32)).astype(BF16)

    @pl.loop(1, PEERS)
    def _(step):
        to = seq_peer(step)
        single(
            term_sent.at[rows_of(to, SHARD)], term_got.at[rows_of(me, SHARD)], 3, (section, to)
        ).start()

    term_got[rows_of(me, SHARD)] = term_sent[rows_of(me, SHARD)]
    exchange(BACK_FIRST, BATCH - 1)
    replicas = 2 * PEERS
    z_span = pl.ds(0, PEERS - 1)
    next_level = (2 * z_peer(1) + core, me)
    reduced = single(kern_sent.at[z_span], kern_got.at[z_span], 5, next_level)
    reduced.wait_recv()
    chunk = kern_got[0].astype(F32)
    for source in range(1, PEERS):
        chunk += kern_got[source].astype(F32)
    kern_all[core, level] = (chunk * (1.0 / math.sqrt(replicas * BATCH))).astype(BF16)

    @pl.loop(1, PEERS)
    def _(step):
        piece = kern_all.at[core, level]
        single(piece, piece, 6, (2 * z_peer(step) + core, me)).start()
    @pl.loop(0, BATCH)
    def _(b):
        here = rows_of(b, ROWS)
        for tile in tiles:
            slope[here, tile] = product(gate[here, :], w[tile, :], ((1,), (1,)))
    spans = pl.ds(0, WIDTH - SHARD)
    scattered = single(term_sent.at[spans], term_got.at[spans], 3, (section, seq_peer(1)))
    scattered.wait_recv()
    rows = term_got[0:SHARD].astype(F32)
    for source in range(1, PEERS):
        rows += term_got[source * SHARD : (source + 1) * SHARD].astype(F32)
    for part in range(9):
        down, across = (part // 3) * 16, (part % 3) * 128
        part_sent[part] = rows[down : down + 16, across : across + 128].astype(BF16)

    @pl.loop(1, PEERS)
    def _(step):
        to = z_peer(step)
        single(part_sent.at[to], part_got.at[level], 7, (2 * to + core, me)).start()

    part_got[level] = part_sent[level]

    def finish(b):
        here = slice(b * ROWS, (b + 1) * ROWS)
        exchanged(BACK_FIRST, b).wait_recv()
        for tile in tiles:
            mix_part = product(mats[IN_RIGHT + 4], got[BACK_FIRST, here, tile])
            grad[here, tile] = (slope[here, tile] + mix_part).astype(BF16)
    finish(0)
    part_reduced = single(part_sent.at[z_span], part_got.at[z_span], 7, next_level)
    part_reduced.wait_recv()
    total = part_got[0].astype(F32)
    for source in range(1, PEERS):
        total += part_got[source].astype(F32)
    part_all[core, level] = (total * (1.0 / math.sqrt(replicas * BATCH * PEERS * ROWS))).astype(BF16)

    @pl.loop(1, PEERS)
    def _(step):
        piece = part_all.at[core, level]
        single(piece, piece, 8, (2 * z_peer(step) + core, me)).start()
    finish(1)
    kern_rest = kern_all.at[core, z_span]
    collected = single(kern_rest, kern_rest, 6, next_level)
    collected.wait_recv()
    kern_half = kern_all.at[core]
    kern_pair = single(kern_half, kern_half, 9, sibling)
    kern_pair.start()
    part_rest = part_all.at[core, z_span]
    part_collected = single(part_rest, part_rest, 8, next_level)
    part_collected.wait_recv()
    part_half = part_all.at[core, pl.ds(0, 9)]
    part_pair = single(part_half, part_half, 10, sibling)
    part_pair.start()
    finish(2)
    kern_pair.wait_recv()
    part_pair.wait_recv()
    for side in range(2):
        for part in range(PEERS):
            down, across = side * (ROWS // 2) + (part // 2) * 16, (part % 2) * HALF
            kernel_out[down : down + 16, across : across + HALF] = kern_all[side, part]
        for part in range(9):
            down, across = (part // 3) * 16, side * HALF + (part % 3) * 128
            weight_out[down : down + 16, across : across + 128] = part_all[side, part].astype(F32)
    for done in (
        gathered,
        paired,
        swapped,
        scattered,
        kern_swap,
        reduced,
        collected,
        part_reduced,
        part_collected,
        kern_pair,
        part_pair,
    ):
        done.wait_send()
    for which in range(4):

        @pl.loop(0, BATCH)
        def _(b):
            exchanged(which, b).wait_send()


def local(
    layer_input,
    grad_out,
    gate_weight,
    mix_in_right,
    mix_in_left,
    mix_out_left,
    mix_out_right,
    kernel,
):
    tokens = BATCH * ROWS
    outside = pl.BlockSpec(memory_space=pltpu.MemorySpace.HBM)
    inside = pl.BlockSpec(memory_space=pltpu.VMEM)
    input_grad, weight_grad, kernel_grad = pl.pallas_call(
        mixer,
        out_shape=(
            jax.ShapeDtypeStruct((tokens, WIDTH), BF16),
            jax.ShapeDtypeStruct((SHARD, WIDTH), F32),
            jax.ShapeDtypeStruct((ROWS, WIDTH), BF16),
        ),
        in_specs=[outside] * 8,
        out_specs=(inside, inside, inside),
        scratch_shapes=[
            pltpu.VMEM((tokens, WIDTH), BF16),
            pltpu.VMEM((tokens, WIDTH), BF16),
            pltpu.VMEM((WIDTH, WIDTH), BF16),
            pltpu.VMEM((ROWS, WIDTH), BF16),
            pltpu.VMEM((4, ROWS, 64), BF16),
            pltpu.VMEM((8, ROWS, ROWS), BF16),
            pltpu.VMEM((4, tokens, WIDTH), BF16),
            pltpu.VMEM((4, tokens, WIDTH), BF16),
            pltpu.VMEM((tokens, WIDTH), F32),
            pltpu.VMEM((tokens, WIDTH), F32),
            pltpu.VMEM((tokens, WIDTH), BF16),
            pltpu.VMEM((ROWS, WIDTH), F32),
            pltpu.VMEM((WIDTH, HALF), F32),
            pltpu.VMEM((WIDTH, HALF), BF16),
            pltpu.VMEM((WIDTH, HALF), BF16),
            pltpu.VMEM((WIDTH, HALF), BF16),
            pltpu.VMEM((WIDTH, HALF), BF16),
            pltpu.VMEM((ROWS // 2, WIDTH), BF16),
            pltpu.VMEM((ROWS // 2, WIDTH), BF16),
            pltpu.VMEM((PEERS, 16, HALF), BF16),
            pltpu.VMEM((PEERS, 16, HALF), BF16),
            pltpu.VMEM((2, PEERS, 16, HALF), BF16),
            pltpu.VMEM((PEERS, 16, 128), BF16),
            pltpu.VMEM((PEERS, 16, 128), BF16),
            pltpu.VMEM((2, PEERS, 16, 128), BF16),
            pltpu.SemaphoreType.DMA((8,)),
            pltpu.SemaphoreType.DMA((4, BATCH)),
            pltpu.SemaphoreType.DMA((4, BATCH)),
            pltpu.SemaphoreType.DMA((11,)),
            pltpu.SemaphoreType.DMA((11,)),
        ],
        compiler_params=pltpu.CompilerParams(
            collective_id=0, has_side_effects=True, vmem_limit_bytes=40 << 20
        ),
    )(
        *(
            pltpu.with_memory_space_constraint(value, pltpu.MemorySpace.HBM)
            for value in (
                layer_input.reshape(tokens, WIDTH),
                grad_out.reshape(tokens, WIDTH),
                gate_weight,
                mix_in_right.reshape(ROWS, 64),
                mix_in_left.reshape(ROWS, 64),
                mix_out_left.reshape(ROWS, 64),
                mix_out_right.reshape(ROWS, 64),
                kernel,
            )
        )
    )
    return (input_grad.reshape(1, BATCH, ROWS, WIDTH), weight_grad, kernel_grad)


def solution(mesh):
    placed = (
        P("section", None, "seq", None),
        P("section", None, "seq", None),
        P("seq", None),
        P("seq", None, None),
        P("seq", None, None),
        P("seq", None, None),
        P("seq", None, None),
        P("seq", None),
    )
    return jax.shard_map(
        local,
        mesh=mesh,
        in_specs=placed,
        out_specs=(P("section", None, "seq", None), P("seq", None), P("seq", None)),
        check_vma=False,
    )
```

time: 116 us -> 103 us (0.89)
  local copies, waits for them, and re-layouts: 8.99 us -> 2.42 us
  Pallas kernels: 106 us -> 99.9 us
    unnamed x15 -> x3, local copies, waits for them, and re-layouts: 8.99 us -> 2.42 us
    pallas_call x1, Pallas kernels: 106 us -> 99.9 us  [local(): pl.pallas_call(mixer, out_shape=(jax.ShapeDtypeStruct((tokens, WIDTH), BF...]
where the time goes in v2:
time: 103 us
  Pallas kernels  99.9 us (97%)
  local copies, waits for them, and re-layouts  2.42 us (2%)
    pallas_call x1, Pallas kernels, local(): pl.pallas_call(mixer, out_shape=(jax.ShapeDtypeStruct((tokens, WIDTH), BF...  99.9 us
    unnamed x3, local copies, waits for them, and re-layouts  2.42 us

profile of v2, /device:TPU:1, one launch (start us, length us, event | category | flops | bytes accessed | tf_op | source)
XLA Modules:
  0.0 103.0 jit_solution(16277860402216413177)
XLA Ops:
  0.6 99.9 %shard_map.103 = (bf16[768,768]{1,0:T(8,128)(2,1)S(1)}, f32[48,768]{1,0:T(8,128)S(1)}, bf16[256,768]{1,0:T(8,128)(2,1)S(1)}) custom-call(bf16[768,768]{1,0:T(8,128)(2,1)} %bitcast.8, bf16[768,768]{1,0:T(8,128)(2,1)} %bitcast.9, bf16[48,768]{1,0:T(8,128)(2,1)} %w_any.1, bf16[256,64]{1,0:T(8,128)(2,1)} %bitcast.10, bf16[256,64]{1,0:T(8,128)(2,1)} %bitcast.11, ...), custom_call_target="tpu_custom_call" | custom-call | tf_op jit(solution)/shard_map/pallas_call | solution.py:392
  100.6 1.0 copy.14
  101.6 0.7 copy.15
  102.3 0.7 copy.16

commit v3 on v2

v3 whole, which is shorter than its diff:
```python
import math

import jax
import jax.numpy as jnp
from jax import lax
from jax.experimental import pallas as pl
from jax.experimental.pallas import tpu as pltpu
from jax.sharding import PartitionSpec as P

MESH = pl.DeviceIdType.MESH
BF16 = jnp.bfloat16
F32 = jnp.float32

PEERS = 16
BATCH = 3
ROWS = 256
WIDTH = 768
HALF = WIDTH // 2
TILE = 256
TILES = WIDTH // TILE
NEAR = 4
BLOCKS = 9
SHARD = WIDTH // PEERS

FIRST, THIRD, BACK_THIRD, BACK_FIRST = 0, 1, 2, 3
IN_RIGHT, IN_LEFT, OUT_LEFT, OUT_RIGHT = 0, 1, 2, 3


def product(left, right, contract=((1,), (0,))):
    return lax.dot_general(left, right, (contract, ((), ())), preferred_element_type=F32)


def rows_of(index, step, size=None):
    return pl.ds(pl.multiple_of(index * step, step), size or step)


def mixer(
    x_any,
    g_any,
    w_any,
    in_right_any,
    in_left_any,
    out_left_any,
    out_right_any,
    kern_any,
    grad,
    weight_out,
    kernel_out,
    x,
    flipped,
    g,
    w,
    kern,
    factors,
    mats,
    sent,
    got,
    second,
    slope,
    gate,
    ksum,
    kern_out,
    kern_in,
    kern_sent,
    kern_got,
    kern_all,
    term,
    term_out,
    term_in,
    term_sent,
    term_got,
    part_sent,
    part_got,
    part_all,
    local_sem,
    send_sem,
    recv_sem,
    one_send,
    one_recv,
    block_send,
    block_recv,
):
    section = lax.axis_index("section")
    me = lax.axis_index("seq")
    core = lax.rem(section, 2)
    level = lax.div(section, 2)
    other = 1 - core
    sibling = (2 * level + other, me)
    parity = lax.rem(level, 2)
    pair = (2 * (level + 1 - 2 * parity) + core, me)

    def seq_peer(step):
        shift = lax.rem(7 * step, PEERS)
        down = lax.rem(lax.div(me, NEAR) + lax.div(shift, NEAR), NEAR)
        return down * NEAR + lax.rem(me + shift, NEAR)

    def z_peer(step):
        return lax.rem(level + step, PEERS)

    group, place = lax.div(level, NEAR), lax.rem(level, NEAR)

    def near_peer(step):
        return group * NEAR + lax.rem(place + step, NEAR)

    def tile_of(index):
        return rows_of(index, TILE)

    def half_tile(index, side):
        return pl.ds(pl.multiple_of(index * TILE + side * 128, 128), 128)

    full = half_tile(2 * parity, core)
    middle = half_tile(1, core)

    def middle_rows(index):
        return pl.ds(pl.multiple_of(index * SHARD + parity * 16, 16), 32)
    barrier = pltpu.get_barrier_semaphore()

    @pl.loop(1, PEERS)
    def _(step):
        pl.semaphore_signal(barrier, inc=1, device_id=(section, seq_peer(step)), device_id_type=MESH)
        pl.semaphore_signal(
            barrier, inc=1, device_id=(2 * z_peer(step) + core, me), device_id_type=MESH
        )

    @pl.loop(0, NEAR)
    def _(step):
        pl.semaphore_signal(
            barrier, inc=1, device_id=(2 * near_peer(step) + other, me), device_id_type=MESH
        )

    loads = [
        pltpu.make_async_copy(source, target, local_sem.at[slot])
        for slot, (source, target) in enumerate(
            (
                (in_right_any, factors.at[IN_RIGHT]),
                (w_any.at[:, full], w.at[rows_of(me, SHARD), full]),
                (w_any.at[rows_of(parity, 16, 32), middle], w.at[middle_rows(me), middle]),
                (x_any, x),
                (in_left_any, factors.at[IN_LEFT]),
                (out_left_any, factors.at[OUT_LEFT]),
                (out_right_any, factors.at[OUT_RIGHT]),
                (g_any, g),
                (kern_any, kern),
            )
        )
    ]
    for load in loads:
        load.start()
    row = lax.broadcasted_iota(jnp.int32, (ROWS, ROWS), 0)
    col = lax.broadcasted_iota(jnp.int32, (ROWS, ROWS), 1)
    small_row = lax.broadcasted_iota(jnp.int32, (64, ROWS), 0)
    small_col = lax.broadcasted_iota(jnp.int32, (64, ROWS), 1)
    order = jnp.where(col == (row & 3) * 64 + (row >> 2), 1.0, 0.0).astype(BF16)
    repeat = jnp.where(small_row == (small_col & 63), 1.0, 0.0).astype(BF16)
    spread = jnp.where(small_row == (small_col >> 4) * 4 + (small_col & 3), 1.0, 0.0).astype(BF16)
    on_block = (row >> 6) == (col >> 6)
    on_spread = (row >> 6) == ((col >> 2) & 3)

    def ordered(slot):
        blocks = jnp.where(on_block, product(factors[slot], repeat), 0.0).astype(BF16)
        matrix = product(order, blocks)
        mats[slot] = matrix.astype(BF16)
        mats[slot + 4] = matrix.T.astype(BF16)

    def spaced(slot):
        matrix = jnp.where(on_spread, product(factors[slot], spread), 0.0)
        mats[slot] = matrix.astype(BF16)
        mats[slot + 4] = matrix.T.astype(BF16)

    loads[0].wait()
    ordered(IN_RIGHT)
    loads[1].wait()
    loads[2].wait()
    loads[3].wait()
    pl.semaphore_wait(barrier, 2 * (PEERS - 1) + NEAR)

    def exchange(which, tile):
        @pl.loop(1, PEERS)
        def _(step):
            to = seq_peer(step)
            pltpu.make_async_remote_copy(
                sent.at[which, tile, to],
                got.at[which, tile, me],
                send_sem.at[which, tile],
                recv_sem.at[which, tile],
                device_id=(section, to),
                device_id_type=MESH,
            ).start()

        got[which, tile, me] = sent[which, tile, me]

    def exchanged(which, tile):
        span = pl.ds(0, PEERS - 1)
        return pltpu.make_async_remote_copy(
            sent.at[which, tile, span],
            got.at[which, tile, span],
            send_sem.at[which, tile],
            recv_sem.at[which, tile],
            device_id=(section, seq_peer(1)),
            device_id_type=MESH,
        )

    def put(which, tile, b, value):
        sent[which, tile, :, b] = value.astype(BF16).reshape(PEERS, 16, TILE)

    def take(which, tile, b):
        return got[which, tile, :, b].reshape(ROWS, TILE)

    def single(source, target, slot, to):
        return pltpu.make_async_remote_copy(
            source, target, one_send.at[slot], one_recv.at[slot], device_id=to, device_id_type=MESH
        )

    spans = [slice(at, at + ROWS) for at in range(0, BATCH * ROWS, ROWS)]
    next_seq = (section, seq_peer(1))
    next_level = (2 * z_peer(1) + core, me)
    z_span = pl.ds(0, PEERS - 1)
    @pl.loop(1, PEERS)
    def _(step):
        piece = w.at[rows_of(me, SHARD), full]
        single(piece, piece, 0, (section, seq_peer(step))).start()
        piece = w.at[middle_rows(me), middle]
        single(piece, piece, 2, (section, seq_peer(step))).start()
    @pl.loop(0, TILES)
    def _(tile):
        for b, here in enumerate(spans):
            put(FIRST, tile, b, product(mats[IN_RIGHT], x[here, tile_of(tile)]))
        exchange(FIRST, tile)
    for load in loads[4:]:
        load.wait()
    spaced(IN_LEFT)
    ordered(OUT_LEFT)
    spaced(OUT_RIGHT)
    for here in spans:
        for tile in spans:
            flipped[tile, here] = x[here, tile].T
    most = w.at[pl.ds(0, WIDTH - SHARD), full]
    gathered = single(most, most, 0, next_seq)
    gathered.wait_recv()
    most = w.at[pl.ds(0, 32 * (PEERS - 1)), middle]
    gathered_middle = single(most, most, 2, next_seq)
    gathered_middle.wait_recv()
    piece = w.at[:, full]
    crossed = single(piece, piece, 3, pair)
    crossed.start()

    @pl.loop(0, PEERS)
    def _(source):
        piece = w.at[pl.ds(pl.multiple_of(source * SHARD + parity * 32, 16), 16), middle]
        single(piece, piece, 4, pair).start()
    crossed.wait_recv()
    some = w.at[pl.ds(0, 16 * PEERS), middle]
    crossed_middle = single(some, some, 4, pair)
    crossed_middle.wait_recv()
    for tile in range(TILES):
        piece = w.at[:, half_tile(tile, core)]
        single(piece, piece, 1, sibling).start()
    half = w.at[:, pl.ds(0, HALF)]
    paired = single(half, half, 1, sibling)
    paired.wait_recv()
    @pl.loop(0, TILES)
    def _(tile):
        for b, here in enumerate(spans):
            preact = product(x[here, :], w[:, tile_of(tile)])
            sigma = jax.nn.sigmoid(preact)
            upstream = g[here, tile_of(tile)].astype(F32)
            slope[here, tile_of(tile)] = upstream * (sigma * (1.0 + preact * (1.0 - sigma)))
            mix_grad = (upstream * (preact * sigma)).astype(BF16)
            put(BACK_THIRD, tile, b, product(mats[OUT_RIGHT + 4], mix_grad))
        exchange(BACK_THIRD, tile)
    @pl.loop(0, TILES)
    def _(tile):
        exchanged(FIRST, tile).wait_recv()
        kernel = kern[:, tile_of(tile)].astype(F32)
        for b, here in enumerate(spans):
            mixed_in = product(mats[IN_LEFT], take(FIRST, tile, b))
            second[here, tile_of(tile)] = mixed_in
            weighted = (mixed_in * kernel).astype(BF16)
            put(THIRD, tile, b, product(mats[OUT_LEFT], weighted))
        exchange(THIRD, tile)

    def back(tile):
        exchanged(BACK_THIRD, tile).wait_recv()
        kernel = kern[:, tile_of(tile)].astype(F32)
        for b, here in enumerate(spans):
            back_second = product(mats[OUT_LEFT + 4], take(BACK_THIRD, tile, b))
            change = second[here, tile_of(tile)] * back_second
            if b == 0:
                ksum[tile] = change
            else:
                ksum[tile] += change
            back_weighted = (back_second * kernel).astype(BF16)
            put(BACK_FIRST, tile, b, product(mats[IN_LEFT + 4], back_weighted))
        kern_out[tile] = ksum[tile, rows_of(other, ROWS // 2)].astype(BF16)
        swap = single(kern_out.at[tile], kern_in.at[tile], 5 + tile, sibling)
        swap.start()
        return swap

    def kern_scatter(tile):
        kern_swaps[tile].wait_recv()
        half_sum = ksum[tile, rows_of(core, ROWS // 2)] + kern_in[tile].astype(F32)
        for part in range(PEERS):
            down, across = (part // 2) * 16, (part % 2) * 128
            kern_sent[tile, part] = half_sum[down : down + 16, across : across + 128].astype(BF16)

        @pl.loop(1, PEERS)
        def _(step):
            to = z_peer(step)
            single(
                kern_sent.at[tile, to], kern_got.at[tile, level], 8 + tile, (2 * to + core, me)
            ).start()

        kern_got[tile, level] = kern_sent[tile, level]

    replicas = 2 * PEERS

    def kern_gather(tile):
        reduced[tile].wait_recv()
        chunk = kern_got[tile, 0].astype(F32)
        for source in range(1, PEERS):
            chunk += kern_got[tile, source].astype(F32)
        kern_all[core, level, tile] = (chunk * (1.0 / math.sqrt(replicas * BATCH))).astype(BF16)

        @pl.loop(1, PEERS)
        def _(step):
            piece = kern_all.at[core, level, tile]
            single(piece, piece, 11, (2 * z_peer(step) + core, me)).start()

    reduced = [
        single(kern_sent.at[tile, z_span], kern_got.at[tile, z_span], 8 + tile, next_level)
        for tile in range(TILES)
    ]
    kern_swaps = [back(0)]
    kern_swaps.append(back(1))
    kern_scatter(0)
    kern_swaps.append(back(2))
    kern_scatter(1)
    kern_scatter(2)

    def mix(tile):
        exchanged(THIRD, tile).wait_recv()
        for b, here in enumerate(spans):
            mixed = product(mats[OUT_RIGHT], take(THIRD, tile, b))
            gate[here, tile_of(tile)] = (mixed * slope[here, tile_of(tile)]).astype(BF16)
        for across in spans:
            term_out[tile, across] = product(
                flipped[across, :], gate[:, half_tile(tile, other)]
            ).astype(BF16)
        swap = single(term_out.at[tile], term_in.at[tile], 12 + tile, sibling)
        swap.start()
        for across in spans:
            term[tile, across] = product(flipped[across, :], gate[:, half_tile(tile, core)])
        return swap

    def term_scatter(tile):
        term_swaps[tile].wait_recv()
        term_sent[tile] = (term[tile] + term_in[tile].astype(F32)).astype(BF16)

        @pl.loop(1, PEERS)
        def _(step):
            to = seq_peer(step)
            single(
                term_sent.at[tile, rows_of(to, SHARD)],
                term_got.at[tile, rows_of(me, SHARD)],
                15 + tile,
                (section, to),
            ).start()

        term_got[tile, rows_of(me, SHARD)] = term_sent[tile, rows_of(me, SHARD)]
    term_swaps = [mix(0)]
    kern_gather(0)
    term_scatter(0)
    term_swaps.append(mix(1))
    kern_gather(1)
    term_scatter(1)
    term_swaps.append(mix(2))
    term_scatter(2)
    kern_gather(2)
    for here in spans:
        for tile in spans:
            slope[here, tile] = product(gate[here, :], w[tile, :], ((1,), (1,)))

    exchange(BACK_FIRST, 0)

    scattered = [
        single(
            term_sent.at[tile, pl.ds(0, WIDTH - SHARD)],
            term_got.at[tile, pl.ds(0, WIDTH - SHARD)],
            15 + tile,
            next_seq,
        )
        for tile in range(TILES)
    ]

    def part_scatter(tile):
        scattered[tile].wait_recv()
        rows = term_got[tile, 0:SHARD].astype(F32)
        for source in range(1, PEERS):
            rows += term_got[tile, source * SHARD : (source + 1) * SHARD].astype(F32)
        for down in range(3):
            part_sent[3 * down + tile] = rows[down * 16 : down * 16 + 16].astype(BF16)

        for block in range(tile, BLOCKS, 3):

            @pl.loop(0, PEERS // NEAR)
            def _(step):
                to = lax.rem(group + step, PEERS // NEAR) * NEAR + block % NEAR

                @pl.when(to != level)
                def _():
                    pltpu.make_async_remote_copy(
                        part_sent.at[block],
                        part_got.at[block // NEAR, level],
                        block_send.at[block],
                        block_recv.at[block // NEAR],
                        device_id=(2 * to + core, me),
                        device_id_type=MESH,
                    ).start()

            @pl.when(place == block % NEAR)
            def _():
                part_got[block // NEAR, level] = part_sent[block]

    def finish(tile):
        exchanged(BACK_FIRST, tile).wait_recv()
        for b, here in enumerate(spans):
            mix_part = product(mats[IN_RIGHT + 4], take(BACK_FIRST, tile, b))
            grad[here, tile_of(tile)] = (slope[here, tile_of(tile)] + mix_part).astype(BF16)
    part_scatter(0)
    part_scatter(1)
    part_scatter(2)
    exchange(BACK_FIRST, 1)
    finish(0)
    exchange(BACK_FIRST, 2)
    def part_gather(slot):
        block = slot * NEAR + place
        pltpu.make_async_remote_copy(
            part_got.at[slot, z_span],
            part_got.at[slot, z_span],
            block_send.at[0],
            block_recv.at[slot],
            device_id=next_level,
            device_id_type=MESH,
        ).wait_recv()
        total = part_got[slot, 0].astype(F32)
        for source in range(1, PEERS):
            total += part_got[slot, source].astype(F32)
        part_all[core, block] = (
            total * (1.0 / math.sqrt(replicas * BATCH * PEERS * ROWS))
        ).astype(BF16)
        piece = part_all.at[core, block]

        @pl.loop(1, NEAR)
        def _(step):
            single(piece, piece, 18, (2 * near_peer(step) + core, me)).start()

        @pl.loop(0, NEAR)
        def _(step):
            single(piece, piece, 18, (2 * near_peer(step) + other, me)).start()

    part_gather(0)
    part_gather(1)

    @pl.when(place == 0)
    def _():
        part_gather(2)
    kern_rest = kern_all.at[core, z_span]
    collected = single(kern_rest, kern_rest, 11, next_level)
    collected.wait_recv()
    kern_half = kern_all.at[core]
    kern_pair = single(kern_half, kern_half, 20, sibling)
    kern_pair.start()
    finish(1)
    kern_pair.wait_recv()
    for side in range(2):
        for part in range(PEERS):
            for tile in range(TILES):
                down, across = side * (ROWS // 2) + (part // 2) * 16, tile * TILE + (part % 2) * 128
                kernel_out[down : down + 16, across : across + 128] = kern_all[side, part, tile]
    finish(2)
    @pl.when(place == 0)
    def _():
        most = kern_all.at[0, pl.ds(0, 5)]
        single(most, most, 18, next_level).wait_recv()

    @pl.when(place != 0)
    def _():
        most = part_got.at[0]
        single(most, most, 18, next_level).wait_recv()
    for side in range(2):
        for part in range(BLOCKS):
            down, across = (part // 3) * 16, (part % 3) * TILE + side * 128
            weight_out[down : down + 16, across : across + 128] = part_all[side, part].astype(F32)
    for done in (
        gathered,
        gathered_middle,
        crossed,
        crossed_middle,
        paired,
        *kern_swaps,
        *reduced,
        *term_swaps,
        *scattered,
        collected,
        kern_pair,
    ):
        done.wait_send()

    for block in range(BLOCKS):

        def block_sent(pieces):
            pltpu.make_async_remote_copy(
                part_sent.at[pl.ds(0, pieces)],
                part_sent.at[pl.ds(0, pieces)],
                block_send.at[block],
                block_recv.at[0],
                device_id=next_level,
                device_id_type=MESH,
            ).wait_send()

        @pl.when(place == block % NEAR)
        def _():
            block_sent(3)

        @pl.when(place != block % NEAR)
        def _():
            block_sent(4)

    @pl.when(place == 0)
    def _():
        most = kern_all.at[0, pl.ds(0, 7)]
        single(most, most, 18, next_level).wait_send()

    @pl.when(place != 0)
    def _():
        most = part_got.at[0, pl.ds(0, 14)]
        single(most, most, 18, next_level).wait_send()

    for which in range(4):

        @pl.loop(0, TILES)
        def _(tile):
            exchanged(which, tile).wait_send()


def local(
    layer_input,
    grad_out,
    gate_weight,
    mix_in_right,
    mix_in_left,
    mix_out_left,
    mix_out_right,
    kernel,
):
    tokens = BATCH * ROWS
    outside = pl.BlockSpec(memory_space=pltpu.MemorySpace.HBM)
    inside = pl.BlockSpec(memory_space=pltpu.VMEM)
    input_grad, weight_grad, kernel_grad = pl.pallas_call(
        mixer,
        out_shape=(
            jax.ShapeDtypeStruct((tokens, WIDTH), BF16),
            jax.ShapeDtypeStruct((SHARD, WIDTH), F32),
            jax.ShapeDtypeStruct((ROWS, WIDTH), BF16),
        ),
        in_specs=[outside] * 8,
        out_specs=(inside, inside, inside),
        scratch_shapes=[
            pltpu.VMEM((tokens, WIDTH), BF16),
            pltpu.VMEM((WIDTH, tokens), BF16),
            pltpu.VMEM((tokens, WIDTH), BF16),
            pltpu.VMEM((WIDTH, WIDTH), BF16),
            pltpu.VMEM((ROWS, WIDTH), BF16),
            pltpu.VMEM((4, ROWS, 64), BF16),
            pltpu.VMEM((8, ROWS, ROWS), BF16),
            pltpu.VMEM((4, TILES, PEERS, BATCH, 16, TILE), BF16),
            pltpu.VMEM((4, TILES, PEERS, BATCH, 16, TILE), BF16),
            pltpu.VMEM((tokens, WIDTH), F32),
            pltpu.VMEM((tokens, WIDTH), F32),
            pltpu.VMEM((tokens, WIDTH), BF16),
            pltpu.VMEM((TILES, ROWS, TILE), F32),
            pltpu.VMEM((TILES, ROWS // 2, TILE), BF16),
            pltpu.VMEM((TILES, ROWS // 2, TILE), BF16),
            pltpu.VMEM((TILES, PEERS, 16, 128), BF16),
            pltpu.VMEM((TILES, PEERS, 16, 128), BF16),
            pltpu.VMEM((2, PEERS, TILES, 16, 128), BF16),
            pltpu.VMEM((TILES, WIDTH, 128), F32),
            pltpu.VMEM((TILES, WIDTH, 128), BF16),
            pltpu.VMEM((TILES, WIDTH, 128), BF16),
            pltpu.VMEM((TILES, WIDTH, 128), BF16),
            pltpu.VMEM((TILES, WIDTH, 128), BF16),
            pltpu.VMEM((BLOCKS, 16, 128), BF16),
            pltpu.VMEM((3, PEERS, 16, 128), BF16),
            pltpu.VMEM((2, BLOCKS, 16, 128), BF16),
            pltpu.SemaphoreType.DMA((9,)),
            pltpu.SemaphoreType.DMA((4, TILES)),
            pltpu.SemaphoreType.DMA((4, TILES)),
            pltpu.SemaphoreType.DMA((21,)),
            pltpu.SemaphoreType.DMA((21,)),
            pltpu.SemaphoreType.DMA((BLOCKS,)),
            pltpu.SemaphoreType.DMA((3,)),
        ],
        compiler_params=pltpu.CompilerParams(
            collective_id=0, has_side_effects=True, vmem_limit_bytes=40 << 20
        ),
    )(
        *(
            pltpu.with_memory_space_constraint(value, pltpu.MemorySpace.HBM)
            for value in (
                layer_input.reshape(tokens, WIDTH),
                grad_out.reshape(tokens, WIDTH),
                gate_weight,
                mix_in_right.reshape(ROWS, 64),
                mix_in_left.reshape(ROWS, 64),
                mix_out_left.reshape(ROWS, 64),
                mix_out_right.reshape(ROWS, 64),
                kernel,
            )
        )
    )
    return (input_grad.reshape(1, BATCH, ROWS, WIDTH), weight_grad, kernel_grad)


def solution(mesh):
    placed = (
        P("section", None, "seq", None),
        P("section", None, "seq", None),
        P("seq", None),
        P("seq", None, None),
        P("seq", None, None),
        P("seq", None, None),
        P("seq", None, None),
        P("seq", None),
    )
    return jax.shard_map(
        local,
        mesh=mesh,
        in_specs=placed,
        out_specs=(P("section", None, "seq", None), P("seq", None), P("seq", None)),
        check_vma=False,
    )
```

time: 103 us -> 87.2 us (0.85)
  Pallas kernels: 99.9 us -> 84 us
    pallas_call x1, Pallas kernels: 99.9 us -> 84 us  [local(): pl.pallas_call(mixer, out_shape=(jax.ShapeDtypeStruct((tokens, WIDTH), BF...]
where the time goes in v3:
time: 87.2 us; the launch traced here: 87 us
  Pallas kernels  84 us (96%)
  local copies, waits for them, and re-layouts  2.42 us (3%)
    pallas_call x1, Pallas kernels, local(): pl.pallas_call(mixer, out_shape=(jax.ShapeDtypeStruct((tokens, WIDTH), BF...  84 us
    unnamed x3, local copies, waits for them, and re-layouts  2.42 us

profile of v3, /device:TPU:1, one launch (start us, length us, event | category | flops | bytes accessed | tf_op | source)
XLA Modules:
  0.0 87.0 jit_solution(13904827593639441267)
XLA Ops:
  0.6 84.0 %shard_map.103 = (bf16[768,768]{1,0:T(8,128)(2,1)S(1)}, f32[48,768]{1,0:T(8,128)S(1)}, bf16[256,768]{1,0:T(8,128)(2,1)S(1)}) custom-call(bf16[768,768]{1,0:T(8,128)(2,1)} %bitcast.8, bf16[768,768]{1,0:T(8,128)(2,1)} %bitcast.9, bf16[48,768]{1,0:T(8,128)(2,1)} %w_any.1, bf16[256,64]{1,0:T(8,128)(2,1)} %bitcast.10, bf16[256,64]{1,0:T(8,128)(2,1)} %bitcast.11, ...), custom_call_target="tpu_custom_call" | custom-call | tf_op jit(solution)/shard_map/pallas_call | solution.py:559
  84.6 1.0 %copy.14 = bf16[1,3,256,768]{3,2,1,0:T(8,128)(2,1)} copy(bf16[1,3,256,768]{3,2,1,0:T(8,128)(2,1)S(1)} %bitcast.7) | data formatting | bytes 2359296
  85.6 0.7 copy.15
  86.3 0.7 copy.16

commit v4 on v3

--- a/solution.py
+++ b/solution.py
@@ -79,6 +79,7 @@
     one_recv,
     block_send,
     block_recv,
+    ready,
 ):
     section = lax.axis_index("section")
     me = lax.axis_index("seq")
@@ -90,12 +91,13 @@
     pair = (2 * (level + 1 - 2 * parity) + core, me)
 
     def seq_peer(step):
-        shift = lax.rem(7 * step, PEERS)
+        shift = lax.rem(7 * (step + core * (PEERS - 2 * step)), PEERS)
         down = lax.rem(lax.div(me, NEAR) + lax.div(shift, NEAR), NEAR)
         return down * NEAR + lax.rem(me + shift, NEAR)
 
     def z_peer(step):
-        return lax.rem(level + step, PEERS)
+        away = lax.div(step, 2) * (1 - 2 * lax.rem(step, 2)) * (1 - 2 * core)
+        return lax.rem(level + PEERS + PEERS // 2 + away, PEERS)
 
     group, place = lax.div(level, NEAR), lax.rem(level, NEAR)
 
@@ -118,15 +120,19 @@
     @pl.loop(1, PEERS)
     def _(step):
         pl.semaphore_signal(barrier, inc=1, device_id=(section, seq_peer(step)), device_id_type=MESH)
-        pl.semaphore_signal(
-            barrier, inc=1, device_id=(2 * z_peer(step) + core, me), device_id_type=MESH
-        )
-
-    @pl.loop(0, NEAR)
-    def _(step):
-        pl.semaphore_signal(
-            barrier, inc=1, device_id=(2 * near_peer(step) + other, me), device_id_type=MESH
-        )
+
+    pl.semaphore_signal(barrier, inc=1, device_id=sibling, device_id_type=MESH)
+
+    def level_to(away):
+        return (2 * lax.rem(level + away, PEERS) + core, me)
+
+    @pl.when(level < PEERS - 1)
+    def _():
+        pl.semaphore_signal(barrier, inc=1, device_id=level_to(1), device_id_type=MESH)
+
+    @pl.when(level > 0)
+    def _():
+        pl.semaphore_signal(barrier, inc=1, device_id=level_to(PEERS - 1), device_id_type=MESH)
 
     loads = [
         pltpu.make_async_copy(source, target, local_sem.at[slot])
@@ -172,7 +178,32 @@
     loads[1].wait()
     loads[2].wait()
     loads[3].wait()
-    pl.semaphore_wait(barrier, 2 * (PEERS - 1) + NEAR)
+    ends = jnp.where(jnp.logical_or(level == 0, level == PEERS - 1), 1, 0)
+    pl.semaphore_wait(barrier, PEERS - 1 + 3 - ends)
+
+    def pass_on(turn):
+        away = 2**turn
+
+        @pl.when(level < PEERS - away)
+        def _():
+            pl.semaphore_signal(ready.at[turn, 0], inc=1, device_id=level_to(away), device_id_type=MESH)
+
+        @pl.when(level >= away)
+        def _():
+            pl.semaphore_signal(
+                ready.at[turn, 1], inc=1, device_id=level_to(PEERS - away), device_id_type=MESH
+            )
+
+    def passed(turn):
+        away = 2**turn
+
+        @pl.when(level >= away)
+        def _():
+            pl.semaphore_wait(ready.at[turn, 0], 1)
+
+        @pl.when(level < PEERS - away)
+        def _():
+            pl.semaphore_wait(ready.at[turn, 1], 1)
 
     def exchange(which, tile):
         @pl.loop(1, PEERS)
@@ -226,6 +257,8 @@
         for b, here in enumerate(spans):
             put(FIRST, tile, b, product(mats[IN_RIGHT], x[here, tile_of(tile)]))
         exchange(FIRST, tile)
+
+    pass_on(0)
     for load in loads[4:]:
         load.wait()
     spaced(IN_LEFT)
@@ -268,6 +301,9 @@
             mix_grad = (upstream * (preact * sigma)).astype(BF16)
             put(BACK_THIRD, tile, b, product(mats[OUT_RIGHT + 4], mix_grad))
         exchange(BACK_THIRD, tile)
+
+    passed(0)
+    pass_on(1)
     @pl.loop(0, TILES)
     def _(tile):
         exchanged(FIRST, tile).wait_recv()
@@ -330,8 +366,14 @@
         single(kern_sent.at[tile, z_span], kern_got.at[tile, z_span], 8 + tile, next_level)
         for tile in range(TILES)
     ]
+
+    passed(1)
+    pass_on(2)
     kern_swaps = [back(0)]
+    passed(2)
+    pass_on(3)
     kern_swaps.append(back(1))
+    passed(3)
     kern_scatter(0)
     kern_swaps.append(back(2))
     kern_scatter(1)
@@ -404,7 +446,7 @@
 
             @pl.loop(0, PEERS // NEAR)
             def _(step):
-                to = lax.rem(group + step, PEERS // NEAR) * NEAR + block % NEAR
+                to = lax.rem(group + 2 + step, PEERS // NEAR) * NEAR + block % NEAR
 
                 @pl.when(to != level)
                 def _():
@@ -541,6 +583,19 @@
         @pl.loop(0, TILES)
         def _(tile):
             exchanged(which, tile).wait_send()
+
+
+def store(grad, weight, kernel, grad_any, weight_any, kernel_any, sems):
+    copies = [
+        pltpu.make_async_copy(source, target, sems.at[slot])
+        for slot, (source, target) in enumerate(
+            ((grad, grad_any), (kernel, kernel_any), (weight, weight_any))
+        )
+    ]
+    for copy in copies:
+        copy.start()
+    for copy in copies:
+        copy.wait()
 
 
 def local(
@@ -599,6 +654,7 @@
             pltpu.SemaphoreType.DMA((21,)),
             pltpu.SemaphoreType.DMA((BLOCKS,)),
             pltpu.SemaphoreType.DMA((3,)),
+            pltpu.SemaphoreType.REGULAR((4, 2)),
         ],
         compiler_params=pltpu.CompilerParams(
             collective_id=0, has_side_effects=True, vmem_limit_bytes=40 << 20
@@ -618,6 +674,18 @@
             )
         )
     )
+    anywhere = pl.BlockSpec(memory_space=pl.ANY)
+    input_grad, weight_grad, kernel_grad = pl.pallas_call(
+        store,
+        out_shape=tuple(
+            jax.ShapeDtypeStruct(value.shape, value.dtype)
+            for value in (input_grad, weight_grad, kernel_grad)
+        ),
+        in_specs=[anywhere] * 3,
+        out_specs=(anywhere,) * 3,
+        scratch_shapes=[pltpu.SemaphoreType.DMA((3,))],
+        compiler_params=pltpu.CompilerParams(vmem_limit_bytes=1 << 20),
+    )(input_grad, weight_grad, kernel_grad)
     return (input_grad.reshape(1, BATCH, ROWS, WIDTH), weight_grad, kernel_grad)
 
 

time: 87.2 us -> 83 us (0.952)
  local copies, waits for them, and re-layouts: 2.42 us -> 0 us
  Pallas kernels: 84 us -> 82.2 us
    pallas_call x1, Pallas kernels: 84 us -> 81 us  [local(): pl.pallas_call(mixer, out_shape=(jax.ShapeDtypeStruct((tokens, WIDTH), BF...]
    unnamed x3 -> x0, local copies, waits for them, and re-layouts: 2.42 us -> none
    pallas_call x0 -> x1, Pallas kernels: none -> 1.21 us  [local(): pl.pallas_call(store, out_shape=tuple((jax.ShapeDtypeStruct(value.shape,...]
where the time goes in v4:
time: 83 us; the launch traced here: 82.8 us
  Pallas kernels  82.2 us (99%)
    pallas_call x1, Pallas kernels, local(): pl.pallas_call(mixer, out_shape=(jax.ShapeDtypeStruct((tokens, WIDTH), BF...  81 us

profile of v4, /device:TPU:1, one launch (start us, length us, event | category | flops | bytes accessed | tf_op | source)
XLA Modules:
  0.0 82.8 jit_solution(1989086243532726068)
XLA Ops:
  0.6 81.0 %shard_map.103 = (bf16[768,768]{1,0:T(8,128)(2,1)S(1)}, f32[48,768]{1,0:T(8,128)S(1)}, bf16[256,768]{1,0:T(8,128)(2,1)S(1)}) custom-call(bf16[768,768]{1,0:T(8,128)(2,1)} %bitcast.7, bf16[768,768]{1,0:T(8,128)(2,1)} %bitcast.8, bf16[48,768]{1,0:T(8,128)(2,1)} %w_any.1, bf16[256,64]{1,0:T(8,128)(2,1)} %bitcast.9, bf16[256,64]{1,0:T(8,128)(2,1)} %bitcast.10, ...), custom_call_target="tpu_custom_call" | custom-call | tf_op jit(solution)/shard_map/pallas_call | solution.py:614
  81.6 1.2 %shard_map.104 = (bf16[768,768]{1,0:T(8,128)(2,1)}, f32[48,768]{1,0:T(8,128)}, bf16[256,768]{1,0:T(8,128)(2,1)}) custom-call(bf16[768,768]{1,0:T(8,128)(2,1)S(1)} %get-tuple-element.9.grad, f32[48,768]{1,0:T(8,128)S(1)} %get-tuple-element.10.weight, bf16[256,768]{1,0:T(8,128)(2,1)S(1)} %get-tuple-element.11.kernel), custom_call_target="tpu_custom_call" | custom-call | tf_op jit(solution)/shard_map/pallas_call | solution.py:678

commit v5 on v4

--- a/solution.py
+++ b/solution.py
@@ -422,8 +422,6 @@
         for tile in spans:
             slope[here, tile] = product(gate[here, :], w[tile, :], ((1,), (1,)))
 
-    exchange(BACK_FIRST, 0)
-
     scattered = [
         single(
             term_sent.at[tile, pl.ds(0, WIDTH - SHARD)],
@@ -471,6 +469,7 @@
     part_scatter(0)
     part_scatter(1)
     part_scatter(2)
+    exchange(BACK_FIRST, 0)
     exchange(BACK_FIRST, 1)
     finish(0)
     exchange(BACK_FIRST, 2)

time: 83 us -> 83 us (level)
  no operation moved by 1% of the time
where the time goes in v5:
time: 83 us; the launch traced here: 82.9 us
  Pallas kernels  82.2 us (99%)
    pallas_call x1, Pallas kernels, local(): pl.pallas_call(mixer, out_shape=(jax.ShapeDtypeStruct((tokens, WIDTH), BF...  81 us

profile of v5, /device:TPU:1, one launch (start us, length us, event | category | flops | bytes accessed | tf_op | source)
XLA Modules:
  0.0 82.9 jit_solution(10116796173402757008)
XLA Ops:
  0.6 81.0 %shard_map.103 = (bf16[768,768]{1,0:T(8,128)(2,1)S(1)}, f32[48,768]{1,0:T(8,128)S(1)}, bf16[256,768]{1,0:T(8,128)(2,1)S(1)}) custom-call(bf16[768,768]{1,0:T(8,128)(2,1)} %bitcast.7, bf16[768,768]{1,0:T(8,128)(2,1)} %bitcast.8, bf16[48,768]{1,0:T(8,128)(2,1)} %w_any.1, bf16[256,64]{1,0:T(8,128)(2,1)} %bitcast.9, bf16[256,64]{1,0:T(8,128)(2,1)} %bitcast.10, ...), custom_call_target="tpu_custom_call" | custom-call | tf_op jit(solution)/shard_map/pallas_call | solution.py:613
  81.6 1.2 %shard_map.104 = (bf16[768,768]{1,0:T(8,128)(2,1)}, f32[48,768]{1,0:T(8,128)}, bf16[256,768]{1,0:T(8,128)(2,1)}) custom-call(bf16[768,768]{1,0:T(8,128)(2,1)S(1)} %get-tuple-element.9.grad, f32[48,768]{1,0:T(8,128)S(1)} %get-tuple-element.10.weight, bf16[256,768]{1,0:T(8,128)(2,1)S(1)} %get-tuple-element.11.kernel), custom_call_target="tpu_custom_call" | custom-call | tf_op jit(solution)/shard_map/pallas_call | solution.py:677
